TPU v7x, 256 devices: a whole 4x4x8 slice. The times are simulated.
256 devices in a mesh: gx: 8 (over z), gy: 16 (over y, x), gz: 2 (over core).
Axes of the slice: x: 4, y: 4, z: 8, core: 2. Of those that a mesh axis runs over, the one named last changes fastest.
Arguments:
- tensor: float32 [1024, 1024, 256], P('gx', 'gy', 'gz'), may hold values from -60 to 60
- factor_a: float32 [1024, 64], P(('gx', 'gy', 'gz')), may hold values from -6 to 6
- factor_b: float32 [1024, 64], P(('gy', 'gx', 'gz')), may hold values from -6 to 6
- factor_c: float32 [256, 64], P(('gz', 'gx', 'gy')), may hold values from -6 to 6
Outputs:
- slope_a: float32 [1024, 64], P(('gx', 'gy', 'gz'))
- slope_b: float32 [1024, 64], P(('gy', 'gx', 'gz'))
- slope_c: float32 [256, 64], P(('gz', 'gx', 'gy'))
All inputs are finite; a program needn't handle non-finite values.
Results may differ from a plain program's by a relative error of at most 0.0003.
Values sent between devices are 32-bit elements; how exact they have to be, the bound alone decides.
No kernel may reach another device: no remote copies, remote signals or barrier semaphores. Data moves between devices by JAX's collectives and lax.ppermute only.
A program may use at most 64 MiB of HBM per device.

v0:
```python
import jax
import jax.numpy as jnp
from jax import lax
from jax.sharding import PartitionSpec as P

STEPS = 2
step_size = 0.1


def gram_local(matrix):
    return jnp.dot(
        matrix.T, matrix, precision=lax.Precision.HIGHEST, preferred_element_type=jnp.float32
    )


def gather_blocks(own_a, own_b, own_c):
    block_a = lax.all_gather(own_a, ("gy", "gz"), axis=0, tiled=True)
    block_b = lax.all_gather(own_b, ("gx", "gz"), axis=0, tiled=True)
    block_c = lax.all_gather(own_c, ("gx", "gy"), axis=0, tiled=True)
    return (block_a, block_b, block_c)


def gram_sums(own_a, own_b, own_c):
    gram_a, gram_b, gram_c = lax.psum(
        (gram_local(own_a), gram_local(own_b), gram_local(own_c)), ("gx", "gy", "gz")
    )
    return (gram_a, gram_b, gram_c)


def partials(tensor, block_a, block_b, block_c):
    highest = lax.Precision.HIGHEST
    along_k = jnp.einsum("ijk,kr->jri", tensor, block_c, precision=highest)
    moment_a = jnp.einsum("jri,jr->ir", along_k, block_b, precision=highest)
    moment_b = jnp.einsum("jri,ir->jr", along_k, block_a, precision=highest)
    along_i = jnp.einsum("ijk,ir->rjk", tensor, block_a, precision=highest)
    moment_c = jnp.einsum("rjk,jr->kr", along_i, block_b, precision=highest)
    return (moment_a, moment_b, moment_c)


def slopes(first, second, third, moment_a, moment_b, moment_c, grams, counts):
    highest = lax.Precision.HIGHEST
    gram_a, gram_b, gram_c = grams
    count_i, count_j, count_k = counts
    slope_a = (jnp.dot(first, gram_b * gram_c, precision=highest) - moment_a) / (count_j * count_k)
    slope_b = (jnp.dot(second, gram_a * gram_c, precision=highest) - moment_b) / (count_i * count_k)
    slope_c = (jnp.dot(third, gram_a * gram_b, precision=highest) - moment_c) / (count_i * count_j)
    return (slope_a, slope_b, slope_c)


def shards(tensor, factor_a, factor_b, factor_c):
    counts = (
        float(tensor.shape[0] * lax.axis_size("gx")),
        float(tensor.shape[1] * lax.axis_size("gy")),
        float(tensor.shape[2] * lax.axis_size("gz")),
    )
    own_a, own_b, own_c = (factor_a, factor_b, factor_c)
    for round_index in range(STEPS):
        block_a, block_b, block_c = gather_blocks(own_a, own_b, own_c)
        grams = gram_sums(own_a, own_b, own_c)
        moment_a, moment_b, moment_c = partials(tensor, block_a, block_b, block_c)
        moment_a = lax.psum_scatter(moment_a, ("gy", "gz"), scatter_dimension=0, tiled=True)
        moment_b = lax.psum_scatter(moment_b, ("gx", "gz"), scatter_dimension=0, tiled=True)
        moment_c = lax.psum_scatter(moment_c, ("gx", "gy"), scatter_dimension=0, tiled=True)
        slope_a, slope_b, slope_c = slopes(
            own_a, own_b, own_c, moment_a, moment_b, moment_c, grams, counts
        )
        if round_index + 1 < STEPS:
            own_a = own_a - step_size * slope_a
            own_b = own_b - step_size * slope_b
            own_c = own_c - step_size * slope_c
    return (slope_a, slope_b, slope_c)


def solution(mesh):
    placed = (
        P("gx", "gy", "gz"),
        P(("gx", "gy", "gz"), None),
        P(("gy", "gx", "gz"), None),
        P(("gz", "gx", "gy"), None),
    )
    return jax.shard_map(
        shards,
        mesh=mesh,
        in_specs=placed,
        out_specs=(
            P(("gx", "gy", "gz"), None),
            P(("gy", "gx", "gz"), None),
            P(("gz", "gx", "gy"), None),
        ),
        check_vma=False,
    )
```

profile of v0, /device:TPU:1, one launch (start us, length us, event | category | flops | bytes accessed | tf_op | source)
XLA Modules:
  0.0 1523.7 jit_solution(15160832706329019883)
XLA Ops:
  7.2 0.0 all-reduce.11.cloned.1.call-start
  7.2 1.0 fusion.29
  8.2 21.6 %all-gather.1 = f32[16,4,64]{2,1,0:T(4,128)S(1)} all-gather(f32[1,4,64]{2,1,0:T(4,128)} %bitcast.117), channel_id=1, replica_groups=mesh['gx'=8,'gy'=16,'gz'=2] {'gx','gz'}, dimensions={0}, use_global_device_ids=true | all-gather | bytes 17408 | tf_op jit(solution)/shard_map/all_gather | solution.py:18
  29.8 284.8 %all-gather = f32[128,1,64]{2,1,0:T(1,128)S(1)} all-gather(f32[1,1,64]{2,1,0:T(1,128)} %bitcast.121), channel_id=1, replica_groups=mesh['gx'=8,'gy'=16,'gz'=2] {'gx','gy'}, dimensions={0}, use_global_device_ids=true | all-gather | bytes 33024 | tf_op jit(solution)/shard_map/all_gather | solution.py:19
  314.7 1.0 fusion.30
  315.7 77.7 %all-gather.2 = f32[32,4,64]{2,1,0:T(4,128)S(1)} all-gather(f32[1,4,64]{2,1,0:T(4,128)} %bitcast.118), channel_id=1, replica_groups=mesh['gx'=8,'gy'=16,'gz'=2] {'gy','gz'}, dimensions={0}, use_global_device_ids=true | all-gather | bytes 33792 | tf_op jit(solution)/shard_map/all_gather | solution.py:17
  393.4 0.1 copy.53
  393.5 0.1 copy.54
  393.5 9.2 fusion.9
  402.8 0.0 copy-start.2
  402.8 0.0 copy-start.5
  402.8 0.0 copy-start
  402.8 0.0 copy-start.4
  402.8 0.0 copy-start.1
  402.8 0.6 multiply_reduce_fusion.3
  403.4 42.5 %all-reduce.1 = f32[64,64]{1,0:T(8,128)S(1)} all-reduce(f32[64,64]{1,0:T(8,128)S(1)} %bitcast.113), channel_id=3, replica_groups=mesh['gx'=8,'gy'=16,'gz'=2] {'gx','gz'}, use_global_device_ids=true, to_apply=%region_4.0.clone | all-reduce | flops 4096 | bytes 32768
  446.0 0.0 copy-done.2
  446.0 0.1 broadcast_multiply_fusion.1
  446.1 0.0 copy-done.5
  446.1 0.6 dynamic-slice.2
  447.3 76.9 %all-reduce.7 = (f32[64,64]{1,0:T(8,128)S(1)}, f32[64,64]{1,0:T(8,128)S(1)}, f32[64,64]{1,0:T(8,128)S(1)}) all-reduce(f32[64,64]{1,0:T(8,128)S(1)} %fusion.29, f32[64,64]{1,0:T(8,128)S(1)} %broadcast_multiply_fusion.1, f32[64,64]{1,0:T(8,128)S(1)} %fusion.30), channel_id=1, replica_groups=mesh['gx'=8,'gy'=16,'gz'=2] {'gx','gy','gz'}, use_global_device_ids=true, to_apply=%region_0.0 | all-reduce | flops 12288 | bytes 98304 | tf_op jit(solution)/shard_map/psum | solution.py:24
  524.2 0.0 copy-done
  524.3 0.1 fusion.14
  524.4 17.3 %all-gather.3 = f32[16,4,64]{2,1,0:T(4,128)S(1)} all-gather(f32[1,4,64]{2,1,0:T(4,128)S(1)} %bitcast.115), channel_id=1, replica_groups=mesh['gx'=8,'gy'=16,'gz'=2] {'gx','gz'}, dimensions={0}, use_global_device_ids=true | all-gather | bytes 17408 | tf_op jit(solution)/shard_map/all_gather | solution.py:18
  541.8 0.1 copy.56
  541.8 0.0 copy-done.4
  541.8 0.6 dynamic-slice
  543.1 0.1 copy.21
  543.2 119.2 %all-reduce = f32[128,64]{1,0:T(8,128)S(1)} all-reduce(f32[128,64]{1,0:T(8,128)S(1)} %bitcast.111), channel_id=2, replica_groups=mesh['gx'=8,'gy'=16,'gz'=2] {'gy','gz'}, use_global_device_ids=true, to_apply=%region_2.0.clone | all-reduce | flops 8192 | bytes 65536
  662.3 0.0 copy-done.1
  662.3 0.1 fusion.17
  662.5 26.8 %all-gather.5 = f32[32,4,64]{2,1,0:T(4,128)S(1)} all-gather(f32[1,4,64]{2,1,0:T(4,128)S(1)} %bitcast.116), channel_id=1, replica_groups=mesh['gx'=8,'gy'=16,'gz'=2] {'gy','gz'}, dimensions={0}, use_global_device_ids=true | all-gather | bytes 33792 | tf_op jit(solution)/shard_map/all_gather | solution.py:17
  689.3 7.2 fusion
  696.5 2.4 multiply_reduce_fusion
  698.9 0.7 copy.52
  699.6 7.2 fusion.2
  706.8 0.0 copy-start.3
  706.8 2.4 multiply_reduce_fusion.2
  709.3 0.7 copy.33
  710.0 0.0 all-reduce.11.cloned.1.call-update
  710.0 0.2 fusion.31
  710.2 0.2 fusion.32
  710.5 0.0 copy-done.3
  710.5 0.6 dynamic-slice.4
  711.1 0.1 copy.55
  711.2 203.8 %all-reduce.11.cloned.1.call-done = (f32[128,64]{1,0:T(8,128)}, f32[128,64]{1,0:T(8,128)}) async-done(((f32[128,64]{1,0:T(8,128)}, f32[128,64]{1,0:T(8,128)}), (f32[128,64]{1,0:T(8,128)}, f32[128,64]{1,0:T(8,128)})) %all-reduce.11.cloned.1.call-update) | async-done | bytes 65552
  914.9 1.5 fusion.19
  916.4 0.1 broadcast_multiply_fusion
  916.5 285.2 %all-gather.4 = f32[128,1,64]{2,1,0:T(1,128)S(1)} all-gather(f32[1,1,64]{2,1,0:T(1,128)S(1)} %bitcast.120), channel_id=1, replica_groups=mesh['gx'=8,'gy'=16,'gz'=2] {'gx','gy'}, dimensions={0}, use_global_device_ids=true | all-gather | bytes 33024 | tf_op jit(solution)/shard_map/all_gather | solution.py:19
  1201.6 9.3 fusion.8
  1210.9 0.6 multiply_reduce_fusion.1
  1211.5 103.3 %all-reduce.4 = f32[64,64]{1,0:T(8,128)S(1)} all-reduce(f32[64,64]{1,0:T(8,128)S(1)} %bitcast.114), channel_id=6, replica_groups=mesh['gx'=8,'gy'=16,'gz'=2] {'gx','gz'}, use_global_device_ids=true, to_apply=%region_10.0.clone | all-reduce | flops 4096 | bytes 32768
  1314.8 0.1 copy.40
  1314.9 121.7 %all-reduce.3 = f32[128,64]{1,0:T(8,128)S(1)} all-reduce(f32[128,64]{1,0:T(8,128)S(1)} %bitcast.112), channel_id=5, replica_groups=mesh['gx'=8,'gy'=16,'gz'=2] {'gy','gz'}, use_global_device_ids=true, to_apply=%region_8.0.clone | all-reduce | flops 8192 | bytes 65536
  1436.6 76.7 %all-reduce.6 = (f32[64,64]{1,0:T(8,128)S(1)}, f32[64,64]{1,0:T(8,128)S(1)}, f32[64,64]{1,0:T(8,128)S(1)}) all-reduce(f32[64,64]{1,0:T(8,128)S(1)} %fusion.31, f32[64,64]{1,0:T(8,128)S(1)} %broadcast_multiply_fusion, f32[64,64]{1,0:T(8,128)S(1)} %fusion.32), channel_id=1, replica_groups=mesh['gx'=8,'gy'=16,'gz'=2] {'gx','gy','gz'}, use_global_device_ids=true, to_apply=%region_5.0 | all-reduce | flops 12288 | bytes 98304 | tf_op jit(solution)/shard_map/psum | solution.py:24
  1513.4 2.0 fusion.20
  1515.4 0.7 fusion.10
  1516.1 0.7 fusion.11
Async XLA Ops:
  7.2 907.8 %all-reduce.11.cloned.1.call-start = ((), (), s32[]{:S(2)}) async-start(), calls=%async_computation | async-start | bytes 262144
  402.8 43.2 %copy-start.2 = (f32[1,64]{1,0:T(1,128)S(1)}, f32[1,64]{1,0:T(1,128)}, u32[]{:S(2)}) copy-start(f32[1,64]{1,0:T(1,128)} %param.7) | copy-start | bytes 772
  402.8 43.3 %copy-start.5 = (u32[256]{0:T(256)S(1)}, u32[256]{0:T(256)}, u32[]{:S(2)}) copy-start(u32[256]{0:T(256)} %constant.32) | copy-start | bytes 3076
  402.8 121.5 %copy-start = (f32[4,64]{1,0:T(4,128)S(1)}, f32[4,64]{1,0:T(4,128)}, u32[]{:S(2)}) copy-start(f32[4,64]{1,0:T(4,128)} %param.6) | copy-start | bytes 3076
  402.8 139.0 %copy-start.4 = (u32[256]{0:T(256)S(1)}, u32[256]{0:T(256)}, u32[]{:S(2)}) copy-start(u32[256]{0:T(256)} %constant.28) | copy-start | bytes 3076
  402.8 259.5 %copy-start.1 = (f32[4,64]{1,0:T(4,128)S(1)}, f32[4,64]{1,0:T(4,128)}, u32[]{:S(2)}) copy-start(f32[4,64]{1,0:T(4,128)} %param.5) | copy-start | bytes 3076
  706.8 3.7 copy-start.3
Sparse Core Ops, SparseCore 0:
  710.1 204.7 all-reduce.10
where the time goes:
time: 1520 us
  blocking collectives  1250 us (82%)
  waiting for transfers between devices  204 us (13%)
  matrix products  40.5 us (3%)
  between operations  15.5 us (1%)
    all_gather x2, blocking collectives, gather_blocks(): block_c = lax.all_gather(own_c, ('gx', 'gy'), axis=0, tiled=True)  570 us
    unnamed x4, blocking collectives  387 us
    unnamed x2, waiting for transfers between devices  204 us
    psum x2, blocking collectives, gram_sums(): lax.psum((gram_local(own_a), gram_local(own_b), gram_local(own_c)), ('gx'...  154 us
    all_gather x2, blocking collectives, gather_blocks(): block_a = lax.all_gather(own_a, ('gy', 'gz'), axis=0, tiled=True)  105 us
    all_gather x2, blocking collectives, gather_blocks(): block_b = lax.all_gather(own_b, ('gx', 'gz'), axis=0, tiled=True)  39 us
  transfers between devices with their start and end apart: 1, of which 1 were waited for; matrix products, arithmetic and copies ran while one was open for 0% of the time, Pallas kernels for 0%

commit v1 on v0

--- a/solution.py
+++ b/solution.py
@@ -22,7 +22,7 @@
 
 def gram_sums(own_a, own_b, own_c):
     gram_a, gram_b, gram_c = lax.psum(
-        (gram_local(own_a), gram_local(own_b), gram_local(own_c)), ("gx", "gy", "gz")
+        lax.psum((gram_local(own_a), gram_local(own_b), gram_local(own_c)), ("gy", "gz")), "gx"
     )
     return (gram_a, gram_b, gram_c)
 

time: 1520 us -> 1280 us (0.84)
  blocking collectives: 1250 us -> 909 us
  waiting for transfers between devices: 204 us -> 288 us
    unnamed x4 -> x2, blocking collectives: 387 us -> 146 us
    psum x2, blocking collectives: 154 us -> 49.5 us  [gram_sums(): lax.psum(lax.psum((gram_local(own_a), gram_local(own_b), gram_local(own_c...]
    psum x0 -> x2, waiting for transfers between devices: none -> 85 us  [gram_sums(): lax.psum((gram_local(own_a), gram_local(own_b), gram_local(own_c)), ('gy'...]
    unnamed x2 -> x4, waiting for transfers between devices: 204 us -> 203 us
  transfers between devices with their start and end apart: 1 -> 3, of which waited for: 1 -> 3; matrix products, arithmetic and copies ran while one was open for 0% -> 1% of each run, Pallas kernels for 0% -> 0%
where the time goes in v1:
time: 1280 us; the launch traced here: 1270 us
  blocking collectives  909 us (71%)
  waiting for transfers between devices  288 us (22%)
  matrix products  44.3 us (3%)
  between operations  15.2 us (1%)
    all_gather x2, blocking collectives, gather_blocks(): block_c = lax.all_gather(own_c, ('gx', 'gy'), axis=0, tiled=True)  570 us
    unnamed x4, waiting for transfers between devices  203 us
    unnamed x2, blocking collectives  146 us
    all_gather x2, blocking collectives, gather_blocks(): block_a = lax.all_gather(own_a, ('gy', 'gz'), axis=0, tiled=True)  100 us
    psum x2, waiting for transfers between devices, gram_sums(): lax.psum((gram_local(own_a), gram_local(own_b), gram_local(own_c)), ('gy'...  85 us
    psum x2, blocking collectives, gram_sums(): lax.psum(lax.psum((gram_local(own_a), gram_local(own_b), gram_local(own_c...  49.5 us
    all_gather x2, blocking collectives, gather_blocks(): block_b = lax.all_gather(own_b, ('gx', 'gz'), axis=0, tiled=True)  43.5 us
  transfers between devices with their start and end apart: 3, of which 3 were waited for; matrix products, arithmetic and copies ran while one was open for 1% of the time, Pallas kernels for 0%

profile of v1, /device:TPU:1, one launch (start us, length us, event | category | flops | bytes accessed | tf_op | source)
XLA Modules:
  0.0 1269.7 jit_solution(9989331689822288282)
XLA Ops:
  7.2 0.0 all-reduce.19.cloned.1.call-start
  7.2 1.4 broadcast_multiply_fusion.1
  8.6 1.6 fusion.29
  10.2 21.6 %all-gather.1 = f32[16,4,64]{2,1,0:T(4,128)S(1)} all-gather(f32[1,4,64]{2,1,0:T(4,128)} %bitcast.117), channel_id=1, replica_groups=mesh['gx'=8,'gy'=16,'gz'=2] {'gx','gz'}, dimensions={0}, use_global_device_ids=true | all-gather | bytes 17408 | tf_op jit(solution)/shard_map/all_gather | solution.py:18
  31.8 1.6 fusion.30
  33.4 284.8 %all-gather = f32[128,1,64]{2,1,0:T(1,128)S(1)} all-gather(f32[1,1,64]{2,1,0:T(1,128)} %bitcast.122), channel_id=1, replica_groups=mesh['gx'=8,'gy'=16,'gz'=2] {'gx','gy'}, dimensions={0}, use_global_device_ids=true | all-gather | bytes 33024 | tf_op jit(solution)/shard_map/all_gather | solution.py:19
  318.2 0.0 copy-start.1
  318.2 9.2 fusion.9
  327.5 0.7 copy.21
  328.2 0.0 all-reduce.19.cloned.1.call-update
  328.2 0.0 all-reduce.15.cloned.1.call-start
  328.3 0.1 copy.54
  328.4 0.0 copy-done.1
  328.4 77.1 %all-gather.2 = f32[32,4,64]{2,1,0:T(4,128)S(1)} all-gather(f32[1,4,64]{2,1,0:T(4,128)S(1)} %bitcast.118), channel_id=1, replica_groups=mesh['gx'=8,'gy'=16,'gz'=2] {'gy','gz'}, dimensions={0}, use_global_device_ids=true | all-gather | bytes 33792 | tf_op jit(solution)/shard_map/all_gather | solution.py:17
  405.5 0.1 copy.53
  405.5 7.2 fusion.2
  412.7 0.0 copy-start.5
  412.8 0.0 copy-start.4
  412.8 0.0 copy-start.3
  412.8 0.0 copy-start
  412.8 2.4 multiply_reduce_fusion.2
  415.2 0.6 multiply_reduce_fusion.3
  415.8 0.0 copy-done.5
  415.9 0.6 dynamic-slice.4
  416.4 0.0 copy-done.4
  416.4 0.6 dynamic-slice.2
  417.0 0.0 copy-done.3
  417.0 0.6 dynamic-slice
  418.9 0.7 copy.33
  419.6 42.5 %all-reduce.1 = f32[64,64]{1,0:T(8,128)S(1)} all-reduce(f32[64,64]{1,0:T(8,128)S(1)} %bitcast.113), channel_id=3, replica_groups=mesh['gx'=8,'gy'=16,'gz'=2] {'gx','gz'}, use_global_device_ids=true, to_apply=%region_7.0.clone | all-reduce | flops 4096 | bytes 32768
  462.1 25.3 %all-reduce.19.cloned.1.call-done = (f32[64,64]{1,0:T(8,128)}, f32[64,64]{1,0:T(8,128)}, f32[128,64]{1,0:T(8,128)}, f32[64,64]{1,0:T(8,128)}) async-done(((f32[64,64]{1,0:T(8,128)}, f32[64,64]{1,0:T(8,128)}, f32[128,64]{1,0:T(8,128)}, f32[64,64]{1,0:T(8,128)}), (f32[64,64]{1,0:T(8,128)}, f32[64,64]{1,0:T(8,128)}, f32[128,64]{1,0:T(8,128)}, f32[64,64]{1,0:T(8,128)})) %all-reduce.19.cloned.1.call-update) | async-done | bytes 81936 | tf_op jit(solution)/shard_map/psum | solution.py:25
  487.5 24.8 %all-reduce.10 = (f32[64,64]{1,0:T(8,128)S(1)}, f32[64,64]{1,0:T(8,128)S(1)}, f32[64,64]{1,0:T(8,128)S(1)}) all-reduce(f32[64,64]{1,0:T(8,128)} %get-tuple-element.9, f32[64,64]{1,0:T(8,128)} %get-tuple-element.10, f32[64,64]{1,0:T(8,128)} %get-tuple-element.12), channel_id=1, replica_groups=mesh['gx'=8,'gy'=16,'gz'=2] {'gx'}, use_global_device_ids=true, to_apply=%region_1.0 | all-reduce | flops 12288 | bytes 98304 | tf_op jit(solution)/shard_map/psum | solution.py:24
  512.2 0.0 copy-done
  512.3 0.1 fusion.14
  512.4 21.9 %all-gather.3 = f32[16,4,64]{2,1,0:T(4,128)S(1)} all-gather(f32[1,4,64]{2,1,0:T(4,128)S(1)} %bitcast.116), channel_id=1, replica_groups=mesh['gx'=8,'gy'=16,'gz'=2] {'gx','gz'}, dimensions={0}, use_global_device_ids=true | all-gather | bytes 17408 | tf_op jit(solution)/shard_map/all_gather | solution.py:18
  534.3 0.1 copy.56
  534.3 0.8 fusion.17
  535.2 0.8 fusion.32
  536.0 23.1 %all-gather.5 = f32[32,4,64]{2,1,0:T(4,128)S(1)} all-gather(f32[1,4,64]{2,1,0:T(4,128)S(1)} %bitcast.115), channel_id=1, replica_groups=mesh['gx'=8,'gy'=16,'gz'=2] {'gy','gz'}, dimensions={0}, use_global_device_ids=true | all-gather | bytes 33792 | tf_op jit(solution)/shard_map/all_gather | solution.py:17
  559.1 7.2 fusion
  566.3 0.0 copy-start.2
  566.3 2.4 multiply_reduce_fusion
  568.7 0.7 copy.52
  569.5 0.0 all-reduce.15.cloned.1.call-update
  569.5 0.0 all-reduce.17.cloned.1.call-start
  569.5 0.8 fusion.31
  570.4 0.1 copy.55
  570.4 202.8 %all-reduce.15.cloned.1.call-done = (f32[128,64]{1,0:T(8,128)}, f32[128,64]{1,0:T(8,128)}) async-done(((f32[128,64]{1,0:T(8,128)}, f32[128,64]{1,0:T(8,128)}), (f32[128,64]{1,0:T(8,128)}, f32[128,64]{1,0:T(8,128)})) %all-reduce.15.cloned.1.call-update) | async-done | bytes 65552
  773.2 0.0 copy-done.2
  773.2 1.5 fusion.19
  774.7 0.7 broadcast_multiply_fusion
  775.4 285.0 %all-gather.4 = f32[128,1,64]{2,1,0:T(1,128)S(1)} all-gather(f32[1,1,64]{2,1,0:T(1,128)S(1)} %bitcast.120), channel_id=1, replica_groups=mesh['gx'=8,'gy'=16,'gz'=2] {'gx','gy'}, dimensions={0}, use_global_device_ids=true | all-gather | bytes 33024 | tf_op jit(solution)/shard_map/all_gather | solution.py:19
  1060.3 9.2 fusion.8
  1069.6 0.7 copy.40
  1070.3 0.0 all-reduce.17.cloned.1.call-update
  1070.3 0.6 multiply_reduce_fusion.1
  1070.9 103.7 %all-reduce.4 = f32[64,64]{1,0:T(8,128)S(1)} all-reduce(f32[64,64]{1,0:T(8,128)S(1)} %bitcast.114), channel_id=6, replica_groups=mesh['gx'=8,'gy'=16,'gz'=2] {'gx','gz'}, use_global_device_ids=true, to_apply=%region_16.0.clone | all-reduce | flops 4096 | bytes 32768
  1174.6 59.6 %all-reduce.17.cloned.1.call-done = (f32[64,64]{1,0:T(8,128)}, f32[64,64]{1,0:T(8,128)}, f32[128,64]{1,0:T(8,128)}, f32[64,64]{1,0:T(8,128)}) async-done(((f32[64,64]{1,0:T(8,128)}, f32[64,64]{1,0:T(8,128)}, f32[128,64]{1,0:T(8,128)}, f32[64,64]{1,0:T(8,128)}), (f32[64,64]{1,0:T(8,128)}, f32[64,64]{1,0:T(8,128)}, f32[128,64]{1,0:T(8,128)}, f32[64,64]{1,0:T(8,128)})) %all-reduce.17.cloned.1.call-update) | async-done | bytes 81936 | tf_op jit(solution)/shard_map/psum | solution.py:25
  1234.3 24.8 %all-reduce.9 = (f32[64,64]{1,0:T(8,128)S(1)}, f32[64,64]{1,0:T(8,128)S(1)}, f32[64,64]{1,0:T(8,128)S(1)}) all-reduce(f32[64,64]{1,0:T(8,128)} %get-tuple-element.5, f32[64,64]{1,0:T(8,128)} %get-tuple-element.6, f32[64,64]{1,0:T(8,128)} %get-tuple-element.8), channel_id=1, replica_groups=mesh['gx'=8,'gy'=16,'gz'=2] {'gx'}, use_global_device_ids=true, to_apply=%region_9.0 | all-reduce | flops 12288 | bytes 98304 | tf_op jit(solution)/shard_map/psum | solution.py:24
  1259.0 0.7 fusion.10
  1259.8 2.0 fusion.20
  1261.7 1.4 fusion.11
Async XLA Ops:
  7.2 480.3 %all-reduce.19.cloned.1.call-start = ((), (), s32[]{:S(2)}) async-start(), calls=%async_computation.2 | async-start | bytes 327680 | tf_op jit(solution)/shard_map/psum | solution.py:25
  318.2 10.1 copy-start.1
  328.2 445.0 %all-reduce.15.cloned.1.call-start = ((), (), s32[]{:S(2)}) async-start(), calls=%async_computation | async-start | bytes 262144
  412.7 3.1 copy-start.5
  412.8 3.7 copy-start.4
  412.8 4.3 copy-start.3
  412.8 99.5 %copy-start = (f32[4,64]{1,0:T(4,128)S(1)}, f32[4,64]{1,0:T(4,128)}, u32[]{:S(2)}) copy-start(f32[4,64]{1,0:T(4,128)} %param.6) | copy-start | bytes 3076
  566.3 206.9 %copy-start.2 = (f32[1,64]{1,0:T(1,128)S(1)}, f32[1,64]{1,0:T(1,128)}, u32[]{:S(2)}) copy-start(f32[1,64]{1,0:T(1,128)} %param.7) | copy-start | bytes 772
  569.5 664.8 %all-reduce.17.cloned.1.call-start = ((), (), s32[]{:S(2)}) async-start(), calls=%async_computation.1 | async-start | bytes 327680 | tf_op jit(solution)/shard_map/psum | solution.py:25
Sparse Core Ops, SparseCore 0:
  328.4 159.0 all-reduce.18
  569.6 203.5 all-reduce.14
  1070.4 163.7 all-reduce.16
